TPU v7x, 512 devices: a whole 4x4x16 slice. The times are simulated.
512 devices in a mesh: dp: 64 (over x, z), ctx: 8 (over y, core).
Axes of the slice: x: 4, y: 4, z: 16, core: 2. Of those that a mesh axis runs over, the one named last changes fastest.
Arguments:
- projections: bfloat16 [131072, 6144], P(('dp', 'ctx')), may hold values from -6 to 6
- block_source: int32 [64, 8, 2], P('dp', 'ctx'), may hold values from 0 to 1023, as said below
- clip_ids: int32 [64, 16], P('dp'), may hold values from 0 to 8, as said below
- out_weight: bfloat16 [2048, 1536], P('dp'), may hold values from -1 to 1
Outputs:
- mixed: bfloat16 [131072, 1536], P(('dp', 'ctx'))
Inputs may be any that keep to these rules, and one draw needn't show every extreme that they name: `block_source`: arrival block a lies on the device numbered a // 2 in dp-major order (dp index a // (2 * 8), ctx index (a // 2) % 8). The block that fills pack block (o, j, l) lies on the device with the same ctx index j and dp index o or o XOR 1. Every arrival block fills exactly one pack block. `clip_ids`: in each pack the clip numbers start at 0, never fall and rise by at most one from block to block; every clip spans 1 to 8 blocks, and in every pack some clip spans exactly 8 blocks.
All inputs are finite; a program needn't handle non-finite values.
Results may differ from a plain program's by a relative error of at most 0.0057.
Values may be sent and summed in bfloat16 or wider, within the bound.
A program may use at most 64 MiB of HBM per device.

v0:
```python
import math
import jax
import jax.numpy as jnp
from jax import lax
from jax.sharding import PartitionSpec as P

HEAD = 128
big_negative = -1e30


def partner(value, axis, bit):
    mask = 2**bit
    pairs = [(source, source ^ mask) for source in range(lax.axis_size(axis))]
    return lax.ppermute(value, axis, pairs)


def soft_weights(scores, allowed):
    masked = jnp.where(allowed, scores, big_negative)
    row_max = jnp.max(masked, axis=-1, keepdims=True)
    exponent = jnp.exp(masked - row_max)
    return (exponent / jnp.sum(exponent, axis=-1, keepdims=True)).astype(jnp.bfloat16)


def attend_dense(queries, key_rows, value_rows, token_clip, scaling):
    token_count, head_count, head_size = queries.shape
    step_size = min(token_count, 512)
    step_count = token_count // step_size
    query_steps = queries.reshape(step_count, step_size, head_count, head_size)
    clip_steps = token_clip.reshape(step_count, step_size)

    def one_step(arguments):
        query_block, clip_block = arguments
        scores = (
            jnp.einsum("qhe,khe->hqk", query_block, key_rows, preferred_element_type=jnp.float32)
            * scaling
        )
        allowed = (clip_block[:, None] == token_clip[None, :])[None]
        weights = soft_weights(scores, allowed)
        return jnp.einsum(
            "hqk,khe->qhe", weights, value_rows, preferred_element_type=jnp.float32
        ).astype(jnp.bfloat16)

    outputs = lax.map(one_step, (query_steps, clip_steps))
    return outputs.reshape(token_count, head_count, head_size)


def body(projections, block_source, clip_ids, out_weight):
    ctx_count = lax.axis_size("ctx")
    local_rows, row_width = projections.shape
    local_blocks = block_source.shape[2]
    block_rows = local_rows // local_blocks
    own_blocks = projections.reshape(local_blocks, block_rows, row_width)
    partner_blocks = partner(own_blocks, "dp", 0)
    source_ids = block_source.reshape(local_blocks)
    from_partner = source_ids // (local_blocks * ctx_count) != lax.axis_index("dp")
    chosen_slot = source_ids % local_blocks + local_blocks * from_partner.astype(jnp.int32)
    candidates = jnp.concatenate([own_blocks, partner_blocks], axis=0)
    packed = jnp.take(candidates, chosen_slot, axis=0)
    local_heads = row_width // (3 * HEAD) // ctx_count
    grouped = packed.reshape(local_rows, ctx_count, local_heads, 3 * HEAD)
    block_clip = clip_ids.reshape(-1)
    token_clip = jnp.repeat(block_clip, block_rows)
    scaling = 1.0 / math.sqrt(HEAD)
    regrouped = lax.all_to_all(grouped, "ctx", split_axis=1, concat_axis=0, tiled=True)
    token_count = regrouped.shape[0]
    item_count = regrouped.shape[2]
    features = regrouped.reshape(token_count, item_count, 3 * HEAD)
    queries = features[:, :, :HEAD]
    key_rows = features[:, :, HEAD : 2 * HEAD]
    value_rows = features[:, :, 2 * HEAD :]
    attended = attend_dense(queries, key_rows, value_rows, token_clip, scaling)
    merged = attended.reshape(local_rows * ctx_count, local_heads * HEAD)
    attention_rows = lax.all_to_all(merged, "ctx", split_axis=0, concat_axis=1, tiled=True)
    result = jnp.dot(
        attention_rows,
        lax.all_gather(out_weight, "dp", axis=0, tiled=True),
        preferred_element_type=jnp.float32,
    )
    return result.astype(jnp.bfloat16)


def solution(mesh):
    return jax.shard_map(
        body,
        mesh=mesh,
        in_specs=(P(("dp", "ctx"), None), P("dp", "ctx", None), P("dp", None), P("dp", None)),
        out_specs=P(("dp", "ctx"), None),
        check_vma=False,
    )
```

profile of v0, /device:TPU:8, one launch (start us, length us, event | category | flops | bytes accessed | tf_op | source)
XLA Modules:
  0.0 276.1 jit_solution(7214846663131477792)
XLA Ops:
  6.5 3.8 %collective-permute-start = (bf16[2,128,6144]{2,1,0:T(8,128)(2,1)}, bf16[2,128,6144]{2,1,0:T(8,128)(2,1)S(1)}, u32[]{:S(2)}, u32[]{:S(2)}) collective-permute-start(bf16[2,128,6144]{2,1,0:T(8,128)(2,1)} %bitcast.87), channel_id=1, source_target_pairs={{0,8},{8,0},{16,24},{24,16},{32,40},{40,32},{48,56},{56,48},{64,72... | collective-permute-start | bytes 9437192 | tf_op jit(solution)/shard_map/ppermute | solution.py:14
  10.4 0.7 fusion.31
  11.0 0.7 compare_and_fusion
  11.8 66.9 %collective-permute-done = bf16[2,128,6144]{2,1,0:T(8,128)(2,1)S(1)} collective-permute-done((bf16[2,128,6144]{2,1,0:T(8,128)(2,1)}, bf16[2,128,6144]{2,1,0:T(8,128)(2,1)S(1)}, u32[]{:S(2)}, u32[]{:S(2)}) %collective-permute-start) | collective-permute-done | bytes 3145760 | tf_op jit(solution)/shard_map/ppermute | solution.py:14
  78.7 5.1 %pad_maximum_fusion = bf16[4,128,6144]{2,1,0:T(8,128)(2,1)} fusion(bf16[2,128,6144]{2,1,0:T(8,128)(2,1)S(1)} %collective-permute-done, bf16[2,128,6144]{2,1,0:T(8,128)(2,1)} %bitcast.88), kind=kLoop, calls=%fused_computation.27 | loop fusion | flops 3145728 | bytes 12582912 | tf_op jit(solution)/shard_map/concatenate | solution.py:57
  83.7 3.5 %gather_fusion = bf16[2,128,6144]{2,1,0:T(8,128)(2,1)S(1)} fusion(bf16[4,128,6144]{2,1,0:T(8,128)(2,1)} %pad_maximum_fusion, s32[1024]{0:T(1024)S(1)} %pad_clamp_fusion), kind=kCustom, calls=%fused_computation | custom fusion | bytes 6291464 | tf_op jit(solution)/shard_map/jit(_take)/gather | solution.py:58
  87.3 3.5 %gather.7 = bf16[256,8,2,384]{3,2,1,0:T(2,128)(2,1)} reshape(bf16[2,128,6144]{2,1,0:T(8,128)(2,1)S(1)} %gather_fusion) | data formatting | bytes 6291456 | tf_op jit(solution)/shard_map/jit(_take)/gather | solution.py:58
  90.8 5.0 %broadcast_select_fusion = bf16[256,8,2,384]{3,2,1,0:T(2,128)(2,1)S(1)} fusion(bf16[256,8,2,384]{3,2,1,0:T(2,128)(2,1)} %gather.7, pred[256]{0:T(512)(128)(4,1)S(1)} %broadcast_bitcast_fusion.2), kind=kLoop, calls=%fused_computation.28 | loop fusion | flops 1572864 | bytes 6291712 | tf_op jit(solution)/shard_map/jit(_take)/select_n | solution.py:58
  95.8 4.1 %copy.12 = bf16[256,8,2,384]{3,2,0,1:T(2,128)(2,1)} copy(bf16[256,8,2,384]{3,2,1,0:T(2,128)(2,1)S(1)} %broadcast_select_fusion) | data formatting | bytes 6291456 | tf_op jit(solution)/shard_map/jit(_take)/select_n | solution.py:58
  99.9 5.0 %all-to-all-start = ((bf16[256,8,2,384]{3,2,0,1:T(2,128)(2,1)}), bf16[256,8,2,384]{3,2,0,1:T(2,128)(2,1)S(1)}, u32[]{:S(2)}, u32[]{:S(2)}) async-start(bf16[256,8,2,384]{3,2,0,1:T(2,128)(2,1)} %copy.12), calls=%async_computation | async-start | bytes 6291456 | tf_op jit(solution)/shard_map/all_to_all | solution.py:64
  104.9 0.7 all-gather.2.cloned.1.call-update
  106.1 0.6 reduce.3
  106.9 35.0 %all-to-all-done = bf16[256,8,2,384]{3,2,0,1:T(2,128)(2,1)S(1)} async-done(((bf16[256,8,2,384]{3,2,0,1:T(2,128)(2,1)}), bf16[256,8,2,384]{3,2,0,1:T(2,128)(2,1)S(1)}, u32[]{:S(2)}, u32[]{:S(2)}) %all-to-all-start) | async-done | bytes 3145760 | tf_op jit(solution)/shard_map/all_to_all | solution.py:64
  141.9 0.6 copy.13
  142.5 1.9 fusion.37
  144.3 53.7 %while.11 = (s32[]{:T(128)}, bf16[4,512,2,128]{3,2,1,0:T(2,128)(2,1)S(1)}, s32[4,512]{1,0:T(4,128)S(1)}, bf16[4,512,2,128]{3,1,0,2:T(8,128)(2,1)}, bf16[2048,2,1...) while((s32[]{:T(128)}, ...), condition=%wide.region_3.4_spmd.clone, body=%wide.region_0.3_spmd.clone.sunk | while | flops 1087506432 | bytes 22051484 | solution.py:43
  144.4 0.7 broadcast_compare_fusion.2
  145.1 7.7 %fusion.51 = (f32[2,512]{1,0:T(2,128)S(1)}, f32[2,512,2048]{2,1,0:T(8,128)}) fusion(pred[512,2048]{1,0:T(8,128)(4,1)S(1)} %broadcast_compare_fusion.2, bf16[2048,2,128]{2,0,1:T(8,128)(2,1)} %get-tuple-element.167, bf16[4,512,2,128]{3,1,0,2:T(8,128)(2,1)} %get-tuple-element.166, s32[]{:T(128)} %get-tuple-element.155), kind=kOutput, calls=%fused_computation.56.clone.1 | convolution fusion | flops 545261568 | bytes 10752512 | tf_op jit(solution)/shard_map/while/body/eval_jaxpr/sub | solution.py:20
  152.7 4.7 %fusion.52 = bf16[1,512,2,128]{3,1,2,0:T(8,128)(2,1)S(1)} fusion(bf16[2048,2,128]{2,0,1:T(8,128)(2,1)S(1)} %get-tuple-element.168, f32[2,512,2048]{2,1,0:T(8,128)} %get-tuple-element.145, f32[2,512]{1,0:T(2,128)S(1)} %get-tuple-element.146), kind=kOutput, calls=%fused_computation.13.clone.1 | convolution fusion | flops 541196288 | bytes 9703424 | tf_op jit(solution)/shard_map/while/body/eval_jaxpr/hqk,khe->qhe/dot_general | solution.py:39
  157.8 0.7 broadcast_compare_fusion.2
  158.5 7.7 %fusion.51 = (f32[2,512]{1,0:T(2,128)S(1)}, f32[2,512,2048]{2,1,0:T(8,128)}) fusion(pred[512,2048]{1,0:T(8,128)(4,1)S(1)} %broadcast_compare_fusion.2, bf16[2048,2,128]{2,0,1:T(8,128)(2,1)} %get-tuple-element.167, bf16[4,512,2,128]{3,1,0,2:T(8,128)(2,1)} %get-tuple-element.166, s32[]{:T(128)} %get-tuple-element.155), kind=kOutput, calls=%fused_computation.56.clone.1 | convolution fusion | flops 545261568 | bytes 10752512 | tf_op jit(solution)/shard_map/while/body/eval_jaxpr/sub | solution.py:20
  166.2 4.7 %fusion.52 = bf16[1,512,2,128]{3,1,2,0:T(8,128)(2,1)S(1)} fusion(bf16[2048,2,128]{2,0,1:T(8,128)(2,1)S(1)} %get-tuple-element.168, f32[2,512,2048]{2,1,0:T(8,128)} %get-tuple-element.145, f32[2,512]{1,0:T(2,128)S(1)} %get-tuple-element.146), kind=kOutput, calls=%fused_computation.13.clone.1 | convolution fusion | flops 541196288 | bytes 9703424 | tf_op jit(solution)/shard_map/while/body/eval_jaxpr/hqk,khe->qhe/dot_general | solution.py:39
  171.3 0.7 broadcast_compare_fusion.2
  171.9 7.7 %fusion.51 = (f32[2,512]{1,0:T(2,128)S(1)}, f32[2,512,2048]{2,1,0:T(8,128)}) fusion(pred[512,2048]{1,0:T(8,128)(4,1)S(1)} %broadcast_compare_fusion.2, bf16[2048,2,128]{2,0,1:T(8,128)(2,1)} %get-tuple-element.167, bf16[4,512,2,128]{3,1,0,2:T(8,128)(2,1)} %get-tuple-element.166, s32[]{:T(128)} %get-tuple-element.155), kind=kOutput, calls=%fused_computation.56.clone.1 | convolution fusion | flops 545261568 | bytes 10752512 | tf_op jit(solution)/shard_map/while/body/eval_jaxpr/sub | solution.py:20
  179.6 4.7 %fusion.52 = bf16[1,512,2,128]{3,1,2,0:T(8,128)(2,1)S(1)} fusion(bf16[2048,2,128]{2,0,1:T(8,128)(2,1)S(1)} %get-tuple-element.168, f32[2,512,2048]{2,1,0:T(8,128)} %get-tuple-element.145, f32[2,512]{1,0:T(2,128)S(1)} %get-tuple-element.146), kind=kOutput, calls=%fused_computation.13.clone.1 | convolution fusion | flops 541196288 | bytes 9703424 | tf_op jit(solution)/shard_map/while/body/eval_jaxpr/hqk,khe->qhe/dot_general | solution.py:39
  184.7 0.7 broadcast_compare_fusion.2
  185.3 7.7 %fusion.51 = (f32[2,512]{1,0:T(2,128)S(1)}, f32[2,512,2048]{2,1,0:T(8,128)}) fusion(pred[512,2048]{1,0:T(8,128)(4,1)S(1)} %broadcast_compare_fusion.2, bf16[2048,2,128]{2,0,1:T(8,128)(2,1)} %get-tuple-element.167, bf16[4,512,2,128]{3,1,0,2:T(8,128)(2,1)} %get-tuple-element.166, s32[]{:T(128)} %get-tuple-element.155), kind=kOutput, calls=%fused_computation.56.clone.1 | convolution fusion | flops 545261568 | bytes 10752512 | tf_op jit(solution)/shard_map/while/body/eval_jaxpr/sub | solution.py:20
  193.0 4.7 %fusion.52 = bf16[1,512,2,128]{3,1,2,0:T(8,128)(2,1)S(1)} fusion(bf16[2048,2,128]{2,0,1:T(8,128)(2,1)S(1)} %get-tuple-element.168, f32[2,512,2048]{2,1,0:T(8,128)} %get-tuple-element.145, f32[2,512]{1,0:T(2,128)S(1)} %get-tuple-element.146), kind=kOutput, calls=%fused_computation.13.clone.1 | convolution fusion | flops 541196288 | bytes 9703424 | tf_op jit(solution)/shard_map/while/body/eval_jaxpr/hqk,khe->qhe/dot_general | solution.py:39
  198.0 0.7 all_to_all.28
  198.7 18.5 %all_to_all.34 = bf16[8,256,256]{2,1,0:T(8,128)(2,1)S(1)} all-to-all(bf16[8,256,256]{2,1,0:T(8,128)(2,1)S(1)} %all_to_all.28), channel_id=1, replica_groups=mesh['dp'=64,'ctx'=8] {'ctx'}, dimensions={0} | all-to-all | bytes 2097152 | tf_op jit(solution)/shard_map/all_to_all | solution.py:73
  217.7 46.0 %all-gather.2.cloned.1.call-done = bf16[2048,1536]{1,0:T(8,128)(2,1)} async-done(((bf16[32,1536]{1,0:T(8,128)(2,1)}), bf16[2048,1536]{1,0:T(8,128)(2,1)}) %all-gather.2.cloned.1.call-update) | async-done | bytes 6291472 | tf_op jit(solution)/shard_map/all_gather | solution.py:76
  263.7 5.5 %convolution_convert_fusion = bf16[256,1536]{1,0:T(8,128)(2,1)} fusion(bf16[256,2048]{0,1:T(8,128)(2,1)S(1)} %bitcast.85, bf16[2048,1536]{1,0:T(8,128)(2,1)} %all-gather.2.cloned.1.call-done), kind=kOutput, calls=%fused_computation.29 | convolution fusion | flops 1611005952 | bytes 8126464 | tf_op jit(solution)/shard_map/dot_general | solution.py:74
  (25 shorter events, 2.8 us)
Async XLA Ops:
  6.5 72.1 %collective-permute-start = (bf16[2,128,6144]{2,1,0:T(8,128)(2,1)}, bf16[2,128,6144]{2,1,0:T(8,128)(2,1)S(1)}, u32[]{:S(2)}, u32[]{:S(2)}) collective-permute-start(bf16[2,128,6144]{2,1,0:T(8,128)(2,1)} %bitcast.87), channel_id=1, source_target_pairs={{0,8},{8,0},{16,24},{24,16},{32,40},{40,32},{48,56},{56,48},{64,72... | collective-permute-start | bytes 9437192 | tf_op jit(solution)/shard_map/ppermute | solution.py:14
  99.9 6.3 %copy-start.1 = (s32[1,16]{1,0:T(1,128)S(1)}, s32[1,16]{1,0:T(1,128)}, u32[]{:S(2)}) copy-start(s32[1,16]{1,0:T(1,128)} %param.8) | copy-start | bytes 196
  99.9 42.0 %all-to-all-start = ((bf16[256,8,2,384]{3,2,0,1:T(2,128)(2,1)}), bf16[256,8,2,384]{3,2,0,1:T(2,128)(2,1)S(1)}, u32[]{:S(2)}, u32[]{:S(2)}) async-start(bf16[256,8,2,384]{3,2,0,1:T(2,128)(2,1)} %copy.12), calls=%async_computation | async-start | bytes 6291456 | tf_op jit(solution)/shard_map/all_to_all | solution.py:64
  104.9 158.8 %all-gather.2.cloned.1.call-start = ((), (), s32[]{:S(2)}) async-start(), calls=%async_computation.2 | async-start | bytes 6389760 | tf_op jit(solution)/shard_map/all_gather | solution.py:76
  142.4 1.9 copy-start
Sparse Core Ops, SparseCore 0:
  108.7 155.0 all-gather.1
where the time goes:
time: 277 us; the launch traced here: 276 us
  waiting for transfers between devices  149 us (54%)
  matrix products  54.9 us (20%)
  blocking collectives  18.5 us (7%)
  local copies, waits for them, and re-layouts  17.1 us (6%)
  other arithmetic  14.6 us (5%)
  between operations  13.5 us (5%)
  starting transfers between devices  8.87 us (3%)
    ppermute x1, waiting for transfers between devices, partner(): return lax.ppermute(value, axis, pairs)  66.9 us
    all_gather x1, waiting for transfers between devices, body(): lax.all_gather(out_weight, 'dp', axis=0, tiled=True)  46 us
    all_to_all x1, waiting for transfers between devices, body(): lax.all_to_all(grouped, 'ctx', split_axis=1, concat_axis=0, tiled=True)  35 us
    sub x4, matrix products, soft_weights(): exponent = jnp.exp(masked - row_max)  30.7 us
    dot_general x4, matrix products, one_step(): jnp.einsum('hqk,khe->qhe', weights, value_rows, preferred_element_type=jn...  18.7 us
    all_to_all x1, blocking collectives, body(): lax.all_to_all(merged, 'ctx', split_axis=0, concat_axis=1, tiled=True)  18.5 us
    gather x2, local copies, waits for them, and re-layouts, body(): packed = jnp.take(candidates, chosen_slot, axis=0)  7.07 us
    select_n x2, other arithmetic, body(): packed = jnp.take(candidates, chosen_slot, axis=0)  5.63 us
  transfers between devices with their start and end apart: 3, of which 3 were waited for; matrix products, arithmetic and copies ran while one was open for 21% of the time, Pallas kernels for 0%

commit v1 on v0

--- a/solution.py
+++ b/solution.py
@@ -73,7 +73,9 @@
     attention_rows = lax.all_to_all(merged, "ctx", split_axis=0, concat_axis=1, tiled=True)
     result = jnp.dot(
         attention_rows,
-        lax.all_gather(out_weight, "dp", axis=0, tiled=True),
+        jnp.concatenate(
+            lax.all_to_all(jnp.stack([out_weight] * lax.axis_size("dp")), "dp", 0, 0), axis=0
+        ),
         preferred_element_type=jnp.float32,
     )
     return result.astype(jnp.bfloat16)

time: 277 us -> 517 us (1.87)
  waiting for transfers between devices: 149 us -> 380 us
  starting transfers between devices: 8.87 us -> 27.3 us
  between operations: 13.5 us -> 0.1 us
    all_to_all x0 -> x1, waiting for transfers between devices: none -> 278 us  [body(): lax.all_to_all(jnp.stack([out_weight] * lax.axis_size('dp')), 'dp', 0, 0)]
    all_gather x1 -> x0, waiting for transfers between devices: 46 us -> none  [body(): lax.all_gather(out_weight, 'dp', axis=0, tiled=True)]
    all_to_all x0 -> x1, starting transfers between devices: none -> 18.6 us  [body(): lax.all_to_all(jnp.stack([out_weight] * lax.axis_size('dp')), 'dp', 0, 0)]
  transfers between devices with their start and end apart: 3 -> 3, of which waited for: 3 -> 3; matrix products, arithmetic and copies ran while one was open for 21% -> 1% of each run, Pallas kernels for 0% -> 0%
where the time goes in v1:
time: 517 us; the launch traced here: 516 us
  waiting for transfers between devices  380 us (74%)
  matrix products  54.9 us (11%)
  starting transfers between devices  27.3 us (5%)
  local copies, waits for them, and re-layouts  20.5 us (4%)
  blocking collectives  18.5 us (4%)
  other arithmetic  14.6 us (3%)
    all_to_all x1, waiting for transfers between devices, body(): lax.all_to_all(jnp.stack([out_weight] * lax.axis_size('dp')), 'dp', 0, 0)  278 us
    ppermute x1, waiting for transfers between devices, partner(): return lax.ppermute(value, axis, pairs)  66.9 us
    all_to_all x1, waiting for transfers between devices, body(): lax.all_to_all(grouped, 'ctx', split_axis=1, concat_axis=0, tiled=True)  35.7 us
    sub x4, matrix products, soft_weights(): exponent = jnp.exp(masked - row_max)  30.7 us
    dot_general x4, matrix products, one_step(): jnp.einsum('hqk,khe->qhe', weights, value_rows, preferred_element_type=jn...  18.7 us
    all_to_all x1, starting transfers between devices, body(): lax.all_to_all(jnp.stack([out_weight] * lax.axis_size('dp')), 'dp', 0, 0)  18.6 us
    all_to_all x1, blocking collectives, body(): lax.all_to_all(merged, 'ctx', split_axis=0, concat_axis=1, tiled=True)  18.5 us
  transfers between devices with their start and end apart: 3, of which 3 were waited for; matrix products, arithmetic and copies ran while one was open for 1% of the time, Pallas kernels for 0%

profile of v1, /device:TPU:8, one launch (start us, length us, event | category | flops | bytes accessed | tf_op | source)
XLA Modules:
  0.0 516.5 jit_solution(18226603314352265200)
XLA Ops:
  0.0 3.8 collective-permute-start
  3.8 0.7 fusion.31
  4.5 0.7 compare_and_fusion
  5.3 66.9 %collective-permute-done = bf16[2,128,6144]{2,1,0:T(8,128)(2,1)S(1)} collective-permute-done((bf16[2,128,6144]{2,1,0:T(8,128)(2,1)}, bf16[2,128,6144]{2,1,0:T(8,128)(2,1)S(1)}, u32[]{:S(2)}, u32[]{:S(2)}) %collective-permute-start) | collective-permute-done | bytes 3145760 | tf_op jit(solution)/shard_map/ppermute | solution.py:14
  72.1 5.1 pad_maximum_fusion
  77.2 3.5 gather_fusion
  80.7 3.5 gather.7
  84.3 5.0 broadcast_select_fusion
  89.3 4.1 copy.12
  93.3 4.9 all-to-all-start
  98.8 0.6 reduce.3
  99.5 35.7 %all-to-all-done = bf16[256,8,2,384]{3,2,0,1:T(2,128)(2,1)S(1)} async-done(((bf16[256,8,2,384]{3,2,0,1:T(2,128)(2,1)}), bf16[256,8,2,384]{3,2,0,1:T(2,128)(2,1)S(1)}, u32[]{:S(2)}, u32[]{:S(2)}) %all-to-all-start) | async-done | bytes 3145760 | tf_op jit(solution)/shard_map/all_to_all | solution.py:64
  135.8 1.9 fusion.37
  137.7 53.6 %while.11 = (s32[]{:T(128)}, bf16[4,512,2,128]{3,2,1,0:T(2,128)(2,1)S(1)}, s32[4,512]{1,0:T(4,128)S(1)}, bf16[4,512,2,128]{3,1,0,2:T(8,128)(2,1)}, bf16[2048,2,1...) while((s32[]{:T(128)}, ...), condition=%wide.region_3.4_spmd.clone, body=%wide.region_0.3_spmd.clone.sunk | while | flops 1087506432 | bytes 22051484 | solution.py:43
  137.8 0.7 broadcast_compare_fusion.2
  138.5 7.7 %fusion.51 = (f32[2,512]{1,0:T(2,128)S(1)}, f32[2,512,2048]{2,1,0:T(8,128)}) fusion(pred[512,2048]{1,0:T(8,128)(4,1)S(1)} %broadcast_compare_fusion.2, bf16[2048,2,128]{2,0,1:T(8,128)(2,1)} %get-tuple-element.167, bf16[4,512,2,128]{3,1,0,2:T(8,128)(2,1)} %get-tuple-element.166, s32[]{:T(128)} %get-tuple-element.155), kind=kOutput, calls=%fused_computation.56.clone.1 | convolution fusion | flops 545261568 | bytes 10752512 | tf_op jit(solution)/shard_map/while/body/eval_jaxpr/sub | solution.py:20
  146.1 4.7 fusion.52
  151.2 0.7 broadcast_compare_fusion.2
  151.9 7.7 %fusion.51 = (f32[2,512]{1,0:T(2,128)S(1)}, f32[2,512,2048]{2,1,0:T(8,128)}) fusion(pred[512,2048]{1,0:T(8,128)(4,1)S(1)} %broadcast_compare_fusion.2, bf16[2048,2,128]{2,0,1:T(8,128)(2,1)} %get-tuple-element.167, bf16[4,512,2,128]{3,1,0,2:T(8,128)(2,1)} %get-tuple-element.166, s32[]{:T(128)} %get-tuple-element.155), kind=kOutput, calls=%fused_computation.56.clone.1 | convolution fusion | flops 545261568 | bytes 10752512 | tf_op jit(solution)/shard_map/while/body/eval_jaxpr/sub | solution.py:20
  159.5 4.7 fusion.52
  164.6 0.7 broadcast_compare_fusion.2
  165.3 7.7 %fusion.51 = (f32[2,512]{1,0:T(2,128)S(1)}, f32[2,512,2048]{2,1,0:T(8,128)}) fusion(pred[512,2048]{1,0:T(8,128)(4,1)S(1)} %broadcast_compare_fusion.2, bf16[2048,2,128]{2,0,1:T(8,128)(2,1)} %get-tuple-element.167, bf16[4,512,2,128]{3,1,0,2:T(8,128)(2,1)} %get-tuple-element.166, s32[]{:T(128)} %get-tuple-element.155), kind=kOutput, calls=%fused_computation.56.clone.1 | convolution fusion | flops 545261568 | bytes 10752512 | tf_op jit(solution)/shard_map/while/body/eval_jaxpr/sub | solution.py:20
  173.0 4.7 fusion.52
  178.0 0.7 broadcast_compare_fusion.2
  178.7 7.7 %fusion.51 = (f32[2,512]{1,0:T(2,128)S(1)}, f32[2,512,2048]{2,1,0:T(8,128)}) fusion(pred[512,2048]{1,0:T(8,128)(4,1)S(1)} %broadcast_compare_fusion.2, bf16[2048,2,128]{2,0,1:T(8,128)(2,1)} %get-tuple-element.167, bf16[4,512,2,128]{3,1,0,2:T(8,128)(2,1)} %get-tuple-element.166, s32[]{:T(128)} %get-tuple-element.155), kind=kOutput, calls=%fused_computation.56.clone.1 | convolution fusion | flops 545261568 | bytes 10752512 | tf_op jit(solution)/shard_map/while/body/eval_jaxpr/sub | solution.py:20
  186.4 4.7 fusion.52
  191.4 0.7 all_to_all.31
  192.1 18.5 %all_to_all.39 = bf16[8,256,256]{2,1,0:T(8,128)(2,1)S(1)} all-to-all(bf16[8,256,256]{2,1,0:T(8,128)(2,1)S(1)} %all_to_all.31), channel_id=1, replica_groups=mesh['dp'=64,'ctx'=8] {'ctx'}, dimensions={0} | all-to-all | bytes 2097152 | tf_op jit(solution)/shard_map/all_to_all | solution.py:73
  210.6 3.4 stack.2
  214.0 18.6 %all-to-all-start.2 = ((bf16[64,32,1536]{2,1,0:T(8,128)(2,1)}), bf16[64,32,1536]{2,1,0:T(8,128)(2,1)}, u32[]{:S(2)}, u32[]{:S(2)}) async-start(bf16[64,32,1536]{2,1,0:T(8,128)(2,1)} %stack.2), calls=%async_computation.2 | async-start | bytes 12582912 | tf_op jit(solution)/shard_map/all_to_all | solution.py:77
  233.1 277.9 %all-to-all-done.2 = bf16[64,32,1536]{2,1,0:T(8,128)(2,1)} async-done(((bf16[64,32,1536]{2,1,0:T(8,128)(2,1)}), bf16[64,32,1536]{2,1,0:T(8,128)(2,1)}, u32[]{:S(2)}, u32[]{:S(2)}) %all-to-all-start.2) | async-done | bytes 6291488 | tf_op jit(solution)/shard_map/all_to_all | solution.py:77
  511.0 5.5 %convolution_convert_fusion = bf16[256,1536]{1,0:T(8,128)(2,1)} fusion(bf16[256,2048]{0,1:T(8,128)(2,1)S(1)} %bitcast.86, bf16[2048,1536]{1,0:T(8,128)(2,1)} %bitcast.14), kind=kOutput, calls=%fused_computation.29 | convolution fusion | flops 1611005952 | bytes 8126464 | tf_op jit(solution)/shard_map/dot_general | solution.py:74
  (27 shorter events, 3.4 us)
Async XLA Ops:
  0.0 72.1 %collective-permute-start = (bf16[2,128,6144]{2,1,0:T(8,128)(2,1)}, bf16[2,128,6144]{2,1,0:T(8,128)(2,1)S(1)}, u32[]{:S(2)}, u32[]{:S(2)}) collective-permute-start(bf16[2,128,6144]{2,1,0:T(8,128)(2,1)} %bitcast.88), channel_id=1, source_target_pairs={{0,8},{8,0},{16,24},{24,16},{32,40},{40,32},{48,56},{56,48},{64,72... | collective-permute-start | bytes 9437192 | tf_op jit(solution)/shard_map/ppermute | solution.py:14
  89.2 9.5 %copy-start.2 = (s32[1,16]{1,0:T(1,128)S(1)}, s32[1,16]{1,0:T(1,128)}, u32[]{:S(2)}) copy-start(s32[1,16]{1,0:T(1,128)} %param.8) | copy-start | bytes 196
  93.3 41.9 %all-to-all-start = ((bf16[256,8,2,384]{3,2,0,1:T(2,128)(2,1)}), bf16[256,8,2,384]{3,2,0,1:T(2,128)(2,1)S(1)}, u32[]{:S(2)}, u32[]{:S(2)}) async-start(bf16[256,8,2,384]{3,2,0,1:T(2,128)(2,1)} %copy.12), calls=%async_computation | async-start | bytes 6291456 | tf_op jit(solution)/shard_map/all_to_all | solution.py:64
  135.8 1.9 copy-start
  137.7 72.8 %copy-start.1 = (bf16[32,1536]{1,0:T(8,128)(2,1)S(1)}, bf16[32,1536]{1,0:T(8,128)(2,1)}, u32[]{:S(2)}) copy-start(bf16[32,1536]{1,0:T(8,128)(2,1)} %param.9) | copy-start | bytes 294916
  214.0 297.0 %all-to-all-start.2 = ((bf16[64,32,1536]{2,1,0:T(8,128)(2,1)}), bf16[64,32,1536]{2,1,0:T(8,128)(2,1)}, u32[]{:S(2)}, u32[]{:S(2)}) async-start(bf16[64,32,1536]{2,1,0:T(8,128)(2,1)} %stack.2), calls=%async_computation.2 | async-start | bytes 12582912 | tf_op jit(solution)/shard_map/all_to_all | solution.py:77
